TPU v7x, 256 devices: a whole 4x4x8 slice. The times are simulated.
256 devices in a mesh: section: 4 (over x_hi, core), feat: 64 (over y, x_lo, z).
Axes of the slice: x: 4 (x_hi: 2, x_lo: 2; x = x_hi * 2 + x_lo), y: 4, z: 8, core: 2. Of those that a mesh axis runs over, the one named last changes fastest.
Arguments:
- residual: bfloat16 [4, 128, 4096], P('section'), may hold values from -6 to 6
- enc_weight: bfloat16 [4, 4096, 16384], P('section', None, 'feat'), may hold values from -0.09375 to 0.09375
- dec_weight: bfloat16 [4, 16384, 4, 4096], P('section', 'feat'), may hold values from -2 to 2
- latent_ids: int32 [4, 128, 64], P('section'), may hold values from 0 to 16383, all different within a row
Outputs:
- written: bfloat16 [4, 4096, 128], P('section', 'feat')
Inputs may be any that keep to these rules, and one draw needn't show every extreme that they name: Each row latent_ids[l, n, :] names 64 different latents.
All inputs are finite; a program needn't handle non-finite values.
Results may differ from a plain program's by a relative error of at most 0.0049.
Values may be sent and summed in bfloat16 or wider, within the bound.
A program may use at most 128 MiB of HBM per device.

v0:
```python
import jax
import jax.numpy as jnp
from jax import lax
from jax.sharding import PartitionSpec as P


def prefix(shard, axis, combine, identity):
    size, here = (lax.axis_size(axis), lax.axis_index(axis))
    everything = lax.all_gather(shard, axis)
    start = jnp.broadcast_to(jnp.asarray(identity, shard.dtype), shard.shape)

    def hop(k, before):
        reached = k < here
        new = combine(before, everything[k])
        return jnp.where(reached, new, before)

    return lax.fori_loop(0, size, hop, start)


def add_terms(earlier, later):
    return earlier + later


def local(residual, enc_weight, dec_weight, latent_ids):
    section_pos = lax.axis_index("section")
    feat_pos = lax.axis_index("feat")
    layers = lax.axis_size("section")
    shard_size = enc_weight.shape[2]
    pre_acts = jnp.dot(residual[0], enc_weight[0], preferred_element_type=jnp.float32)
    local_ids = latent_ids[0] - feat_pos * shard_size
    lane_ids = lax.broadcasted_iota(jnp.int32, (1, 1, shard_size), 2)
    active = jnp.sum((local_ids[:, :, None] == lane_ids).astype(jnp.float32), axis=1)
    latent_acts = (jnp.maximum(pre_acts, 0.0) * active).astype(jnp.bfloat16)
    weights = dec_weight[0]
    targets = lax.broadcasted_iota(jnp.int32, (layers,), 0)
    keep_mask = (targets >= section_pos).astype(jnp.float32)
    summed = lax.psum_scatter(
        jnp.einsum("nf,flc->cln", latent_acts, weights, preferred_element_type=jnp.float32),
        "feat",
        scatter_dimension=0,
        tiled=True,
    )
    partial_value = jnp.transpose(summed, (1, 0, 2))
    partial_value = partial_value * keep_mask[:, None, None]
    before = prefix(partial_value, "section", add_terms, jnp.zeros_like(partial_value))
    own_block = lax.dynamic_index_in_dim(before + partial_value, section_pos, 0, keepdims=True)
    written = own_block.astype(jnp.bfloat16)
    return written


def solution(mesh):
    in_specs = (
        P("section", None, None),
        P("section", None, "feat"),
        P("section", "feat", None, None),
        P("section", None, None),
    )
    out_specs = P("section", "feat", None)
    return jax.shard_map(local, mesh=mesh, in_specs=in_specs, out_specs=out_specs, check_vma=False)
```

profile of v0, /device:TPU:6, one launch (start us, length us, event | category | flops | bytes accessed | tf_op | source)
XLA Modules:
  0.0 682.9 jit_solution(12150620590348420855)
XLA Ops:
  6.5 0.0 copy-start
  6.5 0.0 all-reduce.3.cloned.1.call-start
  6.5 0.9 subtract_bitcast_fusion
  7.5 0.1 copy.16
  7.5 3.1 convert_reduce_fusion
  10.6 0.0 copy-done
  10.6 17.1 %fusion.2 = f32[4096,4,128]{0,2,1:T(8,128)} fusion(bf16[256,4,4096]{2,1,0:T(4,128)(2,1)} %bitcast.35, f32[128,256]{1,0:T(8,128)S(1)} %convert_reduce_fusion, bf16[1,4096,256]{2,1,0:T(8,128)(2,1)S(1)} %copy-done, bf16[1,128,4096]{2,1,0:T(8,128)(2,1)} %param.6), kind=kOutput, calls=%fused_computation.5 | convolution fusion | flops 1342275584 | bytes 20054016 | tf_op jit(solution)/shard_map/nf,flc->cln/dot_general | solution.py:38
  27.7 9.9 %copy.18 = f32[4096,4,128]{2,1,0:T(4,128)} copy(f32[4096,4,128]{0,2,1:T(8,128)} %fusion.2) | data formatting | bytes 16777216 | tf_op jit(solution)/shard_map/nf,flc->cln/transpose | solution.py:38
  37.6 0.0 copy-start.1
  37.6 0.0 all-reduce.3.cloned.1.call-update
  37.6 0.6 copy-done.1
  38.3 0.6 dynamic-slice
  39.5 626.5 %all-reduce.3.cloned.1.call-done = f32[4096,4,128]{2,1,0:T(4,128)} async-done(((f32[4096,4,128]{2,1,0:T(4,128)}), f32[4096,4,128]{2,1,0:T(4,128)}) %all-reduce.3.cloned.1.call-update) | async-done | bytes 8388624
  666.0 1.0 fusion.24
  667.0 8.0 %all-gather = f32[16,64,128]{2,1,0:T(8,128)S(1)} all-gather(f32[4,64,128]{2,1,0:T(8,128)S(1)} %copy.19), channel_id=2, replica_groups=mesh['section'=4,'feat'=64] {'section'}, dimensions={0}, use_global_device_ids=true | all-gather | bytes 655360 | tf_op jit(solution)/shard_map/all_gather | solution.py:9
  675.0 0.3 while.14
  675.3 0.1 copy.20
  675.4 0.1 fusion.26
  675.4 0.6 copy.21
  (7 shorter events, 0.2 us)
Async XLA Ops:
  6.5 4.1 copy-start
  6.5 659.4 %all-reduce.3.cloned.1.call-start = ((), (), s32[]{:S(2)}) async-start(), calls=%async_computation | async-start | bytes 16777216
  37.6 0.7 copy-start.1
Sparse Core Ops, SparseCore 0:
  37.7 628.1 all-reduce.2
where the time goes:
time: 695 us; the launch traced here: 683 us
  waiting for transfers between devices  626 us (90%)
  matrix products  17.1 us (2%)
  between operations  14.1 us (2%)
  local copies, waits for them, and re-layouts  11.9 us (2%)
  blocking collectives  8.01 us (1%)
    unnamed x2, waiting for transfers between devices  626 us
    dot_general x1, matrix products, local(): jnp.einsum('nf,flc->cln', latent_acts, weights, preferred_element_type=jn...  17.1 us
  transfers between devices with their start and end apart: 1, of which 1 were waited for; matrix products, arithmetic and copies ran while one was open for 0% of the time, Pallas kernels for 0%

commit v1 on v0

v1 whole, which is shorter than its diff:
```python
import jax
import jax.numpy as jnp
from jax import lax
from jax.experimental import pallas as pl
from jax.experimental.pallas import tpu as pltpu
from jax.sharding import PartitionSpec as P

MESH = pl.DeviceIdType.MESH
F32, BF16 = jnp.float32, jnp.bfloat16
TOK = 128
LANES = 512
A0, A1, B0, B1 = (0, 32), (32, 32), (64, 32), (96, 32)
B = (64, 64)
ORDER = (2, 1, 3, 0)
NEAR, FAR = 0, 1


def when(cond, run):
    if cond is None:
        run()
    else:
        pl.when(cond)(run)


def kernel(res_hbm, enc_hbm, dec_hbm, ids_hbm, out_ref, res, enc, ids, dec, lhs, acc, core_out, core_in, sent, got,
           z_sum, z_out, z_in, load_sem, send_sem, recv_sem):
    section, feat = lax.axis_index("section"), lax.axis_index("feat")
    core, xh = section % 2, section // 2
    y, xl, z = feat // 16, (feat // 8) % 2, feat % 8
    flip = {0: y, 1: y + 1 - 2 * (y % 2), 2: (y + 2) % 4, 3: 3 - y}

    def device(core_=core, xh_=xh, y_=y, xl_=xl, z_=z):
        return (xh_ * 2 + core_, (y_ * 2 + xl_) * 8 + z_)

    other_core = device(core_=1 - core)
    y_by = {1: device(y_=flip[1]), 3: device(y_=flip[3])}
    x_side = device(xl_=1 - xl)
    x_cross = device(xh_=1 - xh, xl_=1 - xl)
    z_by = {k: device(z_=(z + k) % 8) for k in range(1, 8)}

    barrier = pltpu.get_barrier_semaphore()
    for peer in [other_core, y_by[1], y_by[3], x_side, x_cross] + list(z_by.values()):
        pl.semaphore_signal(barrier, inc=1, device_id=peer, device_id_type=MESH)

    loads = {}

    def load(key, src, dst):
        loads[key] = pltpu.make_async_copy(src, dst, load_sem.at[len(loads)])
        loads[key].start()

    load("ids", ids_hbm.at[0], ids)
    load("res", res_hbm.at[0], res)
    load("enc", enc_hbm.at[0], enc)
    for m in ORDER:
        for r in range(2):
            half = xl if r == 0 else 1 - xl
            for j in range(4):
                load((m, r, j), dec_hbm.at[:, flip[m] * 8 + half * 4 + j], dec.at[m, r, j])

    loads["ids"].wait()
    local_ids = ids[...] - feat * 256
    latent = lax.broadcasted_iota(jnp.int32, (256, TOK), 0)
    active = latent == local_ids[0:1, :]
    for k in range(1, 64):
        active = active | (latent == local_ids[k:k + 1, :])
    active = jnp.where(active, 1.0, 0.0).astype(F32).T
    spread = (lax.broadcasted_iota(jnp.int32, (256, 1024), 1) // 4 == lax.broadcasted_iota(jnp.int32, (256, 1024), 0))
    spread = jnp.where(spread, 1.0, 0.0).astype(BF16)
    loads["res"].wait()
    loads["enc"].wait()
    pre_acts = jnp.dot(res[...], enc[...], preferred_element_type=F32)
    acts = (jnp.maximum(pre_acts, 0.0) * active).astype(BF16)
    acts = jnp.dot(acts, spread, preferred_element_type=F32).astype(BF16)
    place = lax.broadcasted_iota(jnp.int32, (TOK, 1024), 1) % 4
    for row, target in enumerate((1 - core, 3 - core, core, core + 2)):
        lhs[pl.ds(row * TOK, TOK), :] = jnp.where((place == target) & (target >= section), acts, jnp.zeros_like(acts))

    numbers = {}

    def number(key):
        return numbers.setdefault(key, len(numbers))

    pending = []

    def remote(key, src, dst, peer):
        i = number(key)
        return pltpu.make_async_remote_copy(
            src_ref=src, dst_ref=dst, send_sem=send_sem.at[i], recv_sem=recv_sem.at[i], device_id=peer, device_id_type=MESH
        )

    def start(cond, key, src, dst, peer):
        when(cond, lambda: remote(key, src, dst, peer).start())
        pending.append((cond, key, src, dst, peer))

    def arrived(key, src, dst):
        remote(key, src, dst, other_core).wait_recv()

    near_here, far_here = xh == 0, xh == 1

    def rows(piece):
        return pl.ds(piece[0], piece[1])

    def pack(t, m, r, piece):
        sent[t, m, r, rows(piece), :] = acc[t, m, r, rows(piece), :].astype(BF16)

    def take(key, step, t, m, r, piece):
        region = got.at[step, t, m, r, rows(piece), :]
        arrived(key, sent.at[t, m, r, rows(piece), :], region)
        acc[t, m, r, rows(piece), :] += got[step, t, m, r, rows(piece), :].astype(F32)

    def send(cond, key, step, t, m, r, piece, to_m, to_r, peer):
        start(cond, key, sent.at[t, m, r, rows(piece), :], got.at[step, t, to_m, to_r, rows(piece), :], peer)

    BOTH = pl.ds(0, 2)
    Y_PATH = {A0: (1, 3), A1: (3, 1), B0: (1, 3), B1: (3, 1)}

    def y_first(step, t, m, r, piece, name):
        k = Y_PATH[piece][0]
        pack(t, m, r, piece)
        send(None, (name, "y1", piece, m ^ k), step, t, m, r, piece, m ^ k, r, y_by[k])

    def y_second(step, t, r, piece, name):
        k = Y_PATH[piece][1]
        pack(t, k, r, piece)
        send(None, (name, "y2", piece), step, t, k, r, piece, 0, r, y_by[k])

    def multiply(m):
        for r in range(2):
            for j in range(4):
                loads[(m, r, j)].wait()
            for n in range(2):
                w = jnp.concatenate([dec.at[m, r, 2 * n + i].reshape(1024, 128)[...] for i in range(2)], axis=1)
                out = jnp.dot(lhs[...], w, preferred_element_type=F32)
                lanes = pl.ds(n * 256, 256)
                for t in range(2):
                    core_out[t, m, r, :, lanes] = out[t * TOK:(t + 1) * TOK].astype(BF16)
                    acc[t, m, r, :, lanes] = out[(2 + t) * TOK:(3 + t) * TOK]
        for t in (FAR, NEAR):
            start(section == 0 if t == NEAR else section != 3, ("core", t, m), core_out.at[t, m], core_in.at[t, m], other_core)

    def collect(m):
        for t in (FAR, NEAR):
            @pl.when(section == 1 if t == NEAR else section != 2)
            def _():
                arrived(("core", t, m), core_out.at[t, m], core_in.at[t, m])
                acc[t, m] += core_in[t, m].astype(F32)

    def spread_out(m):
        def side(t):
            for piece in (A0, A1):
                if m in (2, Y_PATH[piece][0]):
                    k = Y_PATH[piece][0]
                    pack(t, m, BOTH, piece)
                    send(near_here if t == NEAR else None, ("a", t, "y1", piece, m ^ k), 0, t, m, BOTH, piece, m ^ k, BOTH, y_by[k])

        pack(FAR, m, BOTH, B)
        side(FAR)
        send(None, ("b", "side", m), 0, FAR, m, xh, B0, m, 1 - xh, x_side)
        for r in range(2):
            send(near_here, ("b", "cross", m, 1 - r), 0, FAR, m, r, B1, m, 1 - r, x_cross)

        pack(NEAR, m, 1, B)
        side(NEAR)
        send(near_here, ("b", "near", m), 0, NEAR, m, 1, B, m, 0, x_side)

    pl.semaphore_wait(barrier, 12)
    before = None
    for m in ORDER:
        multiply(m)
        if before is not None:
            collect(before)
            spread_out(before)
        before = m
    collect(before)
    spread_out(before)

    def a_first(t, cond):
        for piece in (A0, A1):
            k1, k2 = Y_PATH[piece]

            def add(m):
                take(("a", t, "y1", piece, m), 0, t, m, BOTH, piece)

            def both():
                add(k2)
                pack(t, k2, BOTH, piece)

            when(cond, both)
            send(cond, ("a", t, "y2", piece), 1, t, k2, BOTH, piece, 0, BOTH, y_by[k2])
            when(cond, lambda: add(0))

    a_first(FAR, None)
    a_first(NEAR, near_here)

    for m in ORDER:
        take(("b", "side", m), 0, FAR, m, 1 - xh, B0)

        @pl.when(far_here)
        def _():
            for r in range(2):
                take(("b", "cross", m, r), 0, FAR, m, r, B1)

        when(near_here, lambda: pack(FAR, m, 1, B0))
        when(far_here, lambda: pack(FAR, m, 1, B1))
        send(near_here, ("b", "cross2", m), 1, FAR, m, 1, B0, m, 0, x_cross)
        send(far_here, ("b", "side2", m), 1, FAR, m, 1, B1, m, 0, x_side)

        @pl.when(near_here)
        def _():
            take(("b", "near", m), 0, NEAR, m, 0, B)

    def a_second(t, cond):
        for piece in (A0, A1):
            when(cond, lambda: take(("a", t, "y2", piece), 1, t, 0, BOTH, piece))

    a_second(FAR, None)
    pack(FAR, 0, BOTH, (0, 64))
    send(None, ("a", "side"), 2, FAR, 0, xh, A0, 0, 1 - xh, x_side)
    for r in range(2):
        send(near_here, ("a", "cross", 1 - r), 2, FAR, 0, r, A1, 0, 1 - r, x_cross)
    a_second(NEAR, near_here)
    pack(NEAR, 0, 1, (0, 64))
    send(near_here, ("a", "near"), 2, NEAR, 0, 1, (0, 64), 0, 0, x_side)

    for m in ORDER:
        @pl.when(far_here)
        def _():
            take(("b", "cross2", m), 1, FAR, m, 0, B0)
            take(("b", "side2", m), 1, FAR, m, 0, B1)

        for piece in (B0, B1):
            if m in (2, Y_PATH[piece][0]):
                y_first(2, xh, m, 0, piece, "b")

    take(("a", "side"), 2, FAR, 0, 1 - xh, A0)

    @pl.when(far_here)
    def _():
        for r in range(2):
            take(("a", "cross", r), 2, FAR, 0, r, A1)

    when(near_here, lambda: pack(FAR, 0, 1, A0))
    when(far_here, lambda: pack(FAR, 0, 1, A1))
    send(near_here, ("a", "cross2"), 3, FAR, 0, 1, A0, 0, 0, x_cross)
    send(far_here, ("a", "side2"), 3, FAR, 0, 1, A1, 0, 0, x_side)

    for piece in (B0, B1):
        k1, k2 = Y_PATH[piece]
        take(("b", "y1", piece, k2), 2, xh, k2, 0, piece)
        y_second(3, xh, 0, piece, "b")
        take(("b", "y1", piece, 0), 2, xh, 0, 0, piece)

    @pl.when(near_here)
    def _():
        take(("a", "near"), 2, NEAR, 0, 0, (0, 64))

    @pl.when(far_here)
    def _():
        take(("a", "cross2"), 3, FAR, 0, 0, A0)
        take(("a", "side2"), 3, FAR, 0, 0, A1)

    for piece in (B0, B1):
        take(("b", "y2", piece), 3, xh, 0, 0, piece)

    turned = acc[xh, 0, 0].T.reshape(8, 64, TOK)
    z_sum[...] = turned
    z_out[...] = turned.astype(BF16)
    for k in (4, 3, 5, 2, 6, 1, 7):
        start(None, ("z", k), z_out.at[(z + k) % 8], z_in.at[k], z_by[k])
    total = z_sum[z]
    for k in (1, 7, 2, 6, 3, 5, 4):
        arrived(("z", k), z_out.at[0], z_in.at[k])
        total = total + z_in[k].astype(F32)
    out_ref[0] = total.astype(BF16)

    for cond, key, src, dst, peer in pending:
        when(cond, lambda: remote(key, src, dst, peer).wait_send())


def local(residual, enc_weight, dec_weight, latent_ids):
    dec = dec_weight[0].reshape(256, 4, 32, 128).transpose(0, 2, 1, 3)
    ids = latent_ids.transpose(0, 2, 1)
    blocks = (2, 4, 2, TOK, LANES)
    return pl.pallas_call(
        kernel,
        out_shape=jax.ShapeDtypeStruct((1, 64, TOK), BF16),
        in_specs=[pl.BlockSpec(memory_space=pl.ANY)] * 4,
        out_specs=pl.BlockSpec(memory_space=pltpu.VMEM),
        scratch_shapes=[
            pltpu.VMEM((TOK, 4096), BF16),
            pltpu.VMEM((4096, 256), BF16),
            pltpu.VMEM((64, TOK), jnp.int32),
            pltpu.VMEM((4, 2, 4, 256, 4, 128), BF16),
            pltpu.VMEM((4 * TOK, 1024), BF16),
            pltpu.VMEM(blocks, F32),
            pltpu.VMEM(blocks, BF16),
            pltpu.VMEM(blocks, BF16),
            pltpu.VMEM(blocks, BF16),
            pltpu.VMEM((4,) + blocks, BF16),
            pltpu.VMEM((8, 64, TOK), F32),
            pltpu.VMEM((8, 64, TOK), BF16),
            pltpu.VMEM((8, 64, TOK), BF16),
            pltpu.SemaphoreType.DMA((40,)),
            pltpu.SemaphoreType.DMA((96,)),
            pltpu.SemaphoreType.DMA((96,)),
        ],
        compiler_params=pltpu.CompilerParams(
            collective_id=0, has_side_effects=True, vmem_limit_bytes=60 * 1024 * 1024
        ),
    )(residual, enc_weight, dec, ids)


def solution(mesh):
    in_specs = (
        P("section", None, None),
        P("section", None, "feat"),
        P("section", "feat", None, None),
        P("section", None, None),
    )
    return jax.shard_map(local, mesh=mesh, in_specs=in_specs, out_specs=P("section", "feat", None), check_vma=False)
```

time: 695 us -> 39.4 us (0.06); the launches traced: 683 us -> 39.1 us
  waiting for transfers between devices: 626 us -> 0 us
  Pallas kernels: 0 us -> 37.8 us
  matrix products: 17.1 us -> 0 us
  between operations: 14.1 us -> 0.01 us
  local copies, waits for them, and re-layouts: 11.9 us -> 1.32 us
  blocking collectives: 8.01 us -> 0 us
    unnamed x2 -> x0, waiting for transfers between devices: 626 us -> none
    pallas_call x0 -> x1, Pallas kernels: none -> 37.8 us  [local(): pl.pallas_call(kernel, out_shape=jax.ShapeDtypeStruct((1, 64, TOK), BF16)...]
    dot_general x1 -> x0, matrix products: 17.1 us -> none  [local(): jnp.einsum('nf,flc->cln', latent_acts, weights, preferred_element_type=jn...]
    transpose x1 -> x0, local copies, waits for them, and re-layouts: 9.88 us -> none  [local(): jnp.einsum('nf,flc->cln', latent_acts, weights, preferred_element_type=jn...]
    all_gather x1 -> x0, blocking collectives: 8.01 us -> none  [prefix(): everything = lax.all_gather(shard, axis)]
  transfers between devices with their start and end apart: 1 -> 0, of which waited for: 1 -> 0; matrix products, arithmetic and copies ran while one was open for 0% -> 0% of each run, Pallas kernels for 0% -> 0%
where the time goes in v1:
time: 39.4 us; the launch traced here: 39.1 us
  Pallas kernels  37.8 us (96%)
  local copies, waits for them, and re-layouts  1.32 us (3%)
    pallas_call x1, Pallas kernels, local(): pl.pallas_call(kernel, out_shape=jax.ShapeDtypeStruct((1, 64, TOK), BF16)...  37.8 us
    unnamed x1, local copies, waits for them, and re-layouts  1.32 us

profile of v1, /device:TPU:6, one launch (start us, length us, event | category | flops | bytes accessed | tf_op | source)
XLA Modules:
  0.0 39.1 jit_solution(8855558304348662374)
XLA Ops:
  0.0 37.8 %shard_map.46 = bf16[1,64,128]{2,1,0:T(8,128)(2,1)} custom-call(bf16[1,128,4096]{2,1,0:T(8,128)(2,1)} %res_hbm.1, bf16[1,4096,256]{2,1,0:T(8,128)(2,1)} %enc_hbm.1, bf16[256,32,4,128]{3,2,1,0:T(4,128)(2,1)} %bitcast.4, s32[1,64,128]{2,1,0:T(8,128)} %bitcast.5), custom_call_target="tpu_custom_call" | custom-call | tf_op jit(solution)/shard_map/pallas_call | solution.py:284
  37.8 1.3 %copy.6 = bf16[1,64,128]{2,1,0:T(8,128)(2,1)} copy(bf16[1,64,128]{2,1,0:T(8,128)(2,1)} %shard_map.46) | data formatting | bytes 32768

commit v2 on v0

v2 whole, which is shorter than its diff:
```python
import jax
import jax.numpy as jnp
from jax import lax
from jax.experimental import pallas as pl
from jax.experimental.pallas import tpu as pltpu
from jax.sharding import PartitionSpec as P

MESH = pl.DeviceIdType.MESH
F32, BF16 = jnp.float32, jnp.bfloat16
TOK = 128
A0, A1, B0, B1 = (0, 32), (32, 32), (64, 32), (96, 32)
A, B = (0, 64), (64, 64)
NEAR, FAR = 0, 1
TILES = (2, 1, 3, 0)
Y_PATH = {A0: (1, 3), A1: (3, 1), B0: (1, 3), B1: (3, 1)}


def when(cond, run):
    if cond is None:
        run()
    else:
        @pl.when(cond)
        def _():
            run()


def rows(piece):
    return pl.ds(piece[0], piece[1])


def kernel(res_hbm, enc_hbm, dec_hbm, ids_hbm, out_ref, res, enc, ids, dec, lhs, acc, core_out, core_in, sent, got,
           z_own, z_out, z_in, load_sem, send_sem, recv_sem):
    section, feat = lax.axis_index("section"), lax.axis_index("feat")
    core, xh = section % 2, section // 2
    y, xl, z = feat // 16, (feat // 8) % 2, feat % 8
    z_pair, z_low = z // 2, z % 2
    flip = {0: y, 1: y + 1 - 2 * (y % 2), 2: (y + 2) % 4, 3: 3 - y}
    near_here, far_here = xh == 0, xh == 1

    def device(core_=core, xh_=xh, y_=y, xl_=xl, z_=z):
        return (xh_ * 2 + core_, (y_ * 2 + xl_) * 8 + z_)

    other_core = device(core_=1 - core)
    y_by = {1: device(y_=flip[1]), 3: device(y_=flip[3])}
    x_side = device(xl_=1 - xl)
    x_cross = device(xh_=1 - xh, xl_=1 - xl)
    tile_of = {p: (z_pair + p) % 4 for p in TILES}
    z_by = {(p, e): device(z_=2 * tile_of[p] + (z_low if e == 0 else 1 - z_low)) for p in TILES for e in range(2)}
    z_by.pop((0, 0))

    barrier = pltpu.get_barrier_semaphore()
    for peer in [other_core, y_by[1], y_by[3], x_side, x_cross] + list(z_by.values()):
        pl.semaphore_signal(barrier, inc=1, device_id=peer, device_id_type=MESH)

    loads = {}

    def load(key, src, dst):
        copy = pltpu.make_async_copy(src, dst, load_sem.at[len(loads)])
        loads[key] = copy
        return copy

    def load_dec(p, t):
        for m in range(4):
            for r in range(2):
                tile = flip[m] * 8 + (xl if r == 0 else 1 - xl) * 4 + tile_of[p]
                load((p, t, m, r), dec_hbm.at[:, tile, t], dec.at[p, t, m, r])
        when(near_here if t == NEAR else None, lambda: [loads[(p, t, m, r)].start() for m in range(4) for r in range(2)])

    load("ids", ids_hbm.at[0], ids).start()
    load("res", res_hbm.at[0], res).start()
    load("enc", enc_hbm.at[0], enc).start()
    for p in TILES:
        load_dec(p, FAR)
        load_dec(p, NEAR)

    for nothing_comes, t in ((section == 0, NEAR), (section == 2, FAR)):
        @pl.when(nothing_comes)
        def _():
            for p in TILES:
                core_in[p, t] = jnp.zeros((4, 2, TOK, 128), BF16)

    loads["ids"].wait()
    local_ids = ids[...] - feat * 256
    latent = lax.broadcasted_iota(jnp.int32, (256, TOK), 0)
    active = latent == local_ids[0:1, :]
    for k in range(1, 64):
        active = active | (latent == local_ids[k:k + 1, :])
    active = jnp.where(active, 1.0, 0.0).astype(F32).T
    spread = (lax.broadcasted_iota(jnp.int32, (256, 512), 1) // 2 == lax.broadcasted_iota(jnp.int32, (256, 512), 0))
    spread = jnp.where(spread, 1.0, 0.0).astype(BF16)
    loads["res"].wait()
    loads["enc"].wait()
    pre_acts = jnp.dot(res[...], enc[...], preferred_element_type=F32)
    acts = (jnp.maximum(pre_acts, 0.0) * active).astype(BF16)
    acts = jnp.dot(acts, spread, preferred_element_type=F32).astype(BF16)
    place = lax.broadcasted_iota(jnp.int32, (TOK, 512), 1) % 2
    for t in range(2):
        for row, low in enumerate((1 - core, core)):
            keep = (place == low) & (2 * t + low >= section)
            lhs[t, pl.ds(row * TOK, TOK), :] = jnp.where(keep, acts, jnp.zeros_like(acts))

    numbers = {}
    pending = []

    def remote(key, src, dst, peer):
        i = numbers.setdefault(key, len(numbers))
        return pltpu.make_async_remote_copy(
            src_ref=src, dst_ref=dst, send_sem=send_sem.at[i], recv_sem=recv_sem.at[i], device_id=peer, device_id_type=MESH
        )

    def send(cond, key, src, dst, peer):
        when(cond, lambda: remote(key, src, dst, peer).start())
        pending.append((cond, key, src, dst, peer))

    def arrived(key, region):
        remote(key, region, region, other_core).wait_recv()

    ALL, BOTH = pl.ds(0, 4), pl.ds(0, 2)

    def out(p, t, m, r, piece):
        return sent.at[p, t, m, r, rows(piece), :]

    def slot(step, p, t, m, r, piece):
        return got.at[step, p, t, m, r, rows(piece), :]

    def have(p, t, m, r, piece):
        return acc[p, t, m, r, rows(piece), :]

    def came(step, p, t, m, r, piece):
        return got[step, p, t, m, r, rows(piece), :].astype(F32)

    def keep(p, t, m, r, piece, value):
        acc[p, t, m, r, rows(piece), :] = value

    def pack(p, t, m, r, piece, value):
        sent[p, t, m, r, rows(piece), :] = value.astype(BF16)

    def multiply(p):
        def one(t):
            for m in range(4):
                for r in range(2):
                    loads[(p, t, m, r)].wait()
                w = jnp.concatenate([dec.at[p, t, m, r].reshape(512, 128)[...] for r in range(2)], axis=1)
                both = jnp.dot(lhs[t], w, preferred_element_type=F32)
                for r in range(2):
                    core_out[p, t, m, r] = both[0:TOK, r * 128:(r + 1) * 128].astype(BF16)
                    acc[p, t, m, r] = both[TOK:2 * TOK, r * 128:(r + 1) * 128]

        one(FAR)
        send(section != 3, (p, "core", FAR), core_out.at[p, FAR], core_in.at[p, FAR], other_core)
        when(near_here, lambda: one(NEAR))
        send(section == 0, (p, "core", NEAR), core_out.at[p, NEAR], core_in.at[p, NEAR], other_core)

    FIRST = {A0: 1, A1: 2, B0: 1, B1: 2}
    SLOT_OF = {A0: (0, 3), A1: (1, 0), B0: (0, 3), B1: (1, 0)}

    def y_one(cond, key, step, p, t, r, piece):
        send(cond, key, sent.at[p, t, pl.ds(FIRST[piece], 2), r, rows(piece), :],
             got.at[step, p, t, BOTH, r, rows(piece), :], y_by[Y_PATH[piece][0]])

    def y_two(cond, key, step, p, t, r, piece):
        k = Y_PATH[piece][1]
        send(cond, key, out(p, t, k, r, piece), slot(step, p, t, 0, r, piece), y_by[k])

    def first(p):
        def core_sum(t, m, r, piece):
            return have(p, t, m, r, piece) + core_in[p, t, m, r, rows(piece), :].astype(F32)

        def a_rows(t):
            for piece in (A0, A1):
                for m in range(4):
                    value = core_sum(t, m, BOTH, piece)
                    if m in (FIRST[piece], FIRST[piece] + 1):
                        pack(p, t, m, BOTH, piece, value)
                    else:
                        keep(p, t, m, BOTH, piece, value)

        def b_far():
            for m in range(4):
                value = core_sum(FAR, m, BOTH, B)
                pack(p, FAR, m, BOTH, B, value)
                keep(p, FAR, m, BOTH, B, value)

        def b_near():
            for m in range(4):
                pack(p, NEAR, m, 1, B, core_sum(NEAR, m, 1, B))
                keep(p, NEAR, m, 0, B, core_sum(NEAR, m, 0, B))

        when(section != 2, lambda: arrived((p, "core", FAR), core_in.at[p, FAR]))
        b_far()
        send(None, (p, "b side"), out(p, FAR, ALL, xh, B0), slot(0, p, FAR, ALL, 1 - xh, B0), x_side)
        for r in range(2):
            send(near_here, (p, "b cross", 1 - r), out(p, FAR, ALL, r, B1), slot(0, p, FAR, ALL, 1 - r, B1), x_cross)
        a_rows(FAR)
        for piece in (A0, A1):
            y_one(None, (p, "a y1", FAR, piece), 0, p, FAR, BOTH, piece)
        when(section == 1, lambda: arrived((p, "core", NEAR), core_in.at[p, NEAR]))
        when(near_here, b_near)
        send(near_here, (p, "b near"), out(p, NEAR, ALL, 1, B), slot(0, p, NEAR, ALL, 0, B), x_side)
        when(near_here, lambda: a_rows(NEAR))
        for piece in (A0, A1):
            y_one(near_here, (p, "a y1", NEAR, piece), 0, p, NEAR, BOTH, piece)

    def a_second(p, t, cond):
        for piece in (A0, A1):
            key = (p, "a y1", t, piece)
            k = Y_PATH[piece][1]
            s = SLOT_OF[piece].index(k)

            def go():
                arrived(key, got.at[0, p, t, BOTH, BOTH, rows(piece), :])
                pack(p, t, k, BOTH, piece, have(p, t, k, BOTH, piece) + came(0, p, t, s, BOTH, piece))

            when(cond, go)
            y_two(cond, (p, "a y2", t, piece), 1, p, t, BOTH, piece)

    def b_y_first(p, t, cond):
        for piece in (B0, B1):
            when(cond, lambda: [pack(p, t, m, 0, piece, have(p, t, m, 0, piece)) for m in (FIRST[piece], FIRST[piece] + 1)])
            y_one(cond, (p, "b y1", piece), 2, p, t, 0, piece)

    def b_y_second(p, t, cond):
        for piece in (B0, B1):
            k = Y_PATH[piece][1]
            s = SLOT_OF[piece].index(k)

            def go():
                arrived((p, "b y1", piece), got.at[2, p, t, BOTH, 0, rows(piece), :])
                pack(p, t, k, 0, piece, have(p, t, k, 0, piece) + came(2, p, t, s, 0, piece))

            when(cond, go)
            y_two(cond, (p, "b y2", piece), 3, p, t, 0, piece)

    def b_final(p, t):
        total = []
        for piece in (B0, B1):
            arrived((p, "b y2", piece), slot(3, p, t, 0, 0, piece))
            s = SLOT_OF[piece].index(0)
            total.append(have(p, t, 0, 0, piece) + came(2, p, t, s, 0, piece) + came(3, p, t, 0, 0, piece))
        return total

    def a_y_sum(p, t, piece, r):
        s = SLOT_OF[piece].index(0)
        return have(p, t, 0, r, piece) + came(0, p, t, s, r, piece) + came(1, p, t, 0, r, piece)

    def second(p):
        arrived((p, "b side"), slot(0, p, FAR, ALL, 1 - xh, B0))

        def far_near():
            pack(p, FAR, ALL, 1, B0, have(p, FAR, ALL, 1, B0) + came(0, p, FAR, ALL, 1, B0))

        def far_far():
            keep(p, FAR, ALL, 0, B0, have(p, FAR, ALL, 0, B0) + came(0, p, FAR, ALL, 0, B0))
            for r in range(2):
                arrived((p, "b cross", r), slot(0, p, FAR, ALL, r, B1))
            pack(p, FAR, ALL, 1, B1, have(p, FAR, ALL, 1, B1) + came(0, p, FAR, ALL, 1, B1))
            keep(p, FAR, ALL, 0, B1, have(p, FAR, ALL, 0, B1) + came(0, p, FAR, ALL, 0, B1))

        when(near_here, far_near)
        send(near_here, (p, "b cross2"), out(p, FAR, ALL, 1, B0), slot(1, p, FAR, ALL, 0, B0), x_cross)
        when(far_here, far_far)
        send(far_here, (p, "b side2"), out(p, FAR, ALL, 1, B1), slot(1, p, FAR, ALL, 0, B1), x_side)
        a_second(p, FAR, None)

        def near_near():
            arrived((p, "b near"), slot(0, p, NEAR, ALL, 0, B))
            keep(p, NEAR, ALL, 0, B, have(p, NEAR, ALL, 0, B) + came(0, p, NEAR, ALL, 0, B))

        when(near_here, near_near)
        b_y_first(p, NEAR, near_here)
        a_second(p, NEAR, near_here)

    def third(p):
        def b_far():
            arrived((p, "b cross2"), slot(1, p, FAR, ALL, 0, B0))
            arrived((p, "b side2"), slot(1, p, FAR, ALL, 0, B1))
            keep(p, FAR, ALL, 0, B, have(p, FAR, ALL, 0, B) + came(1, p, FAR, ALL, 0, B))

        when(far_here, b_far)
        b_y_first(p, FAR, far_here)

        for piece in (A0, A1):
            arrived((p, "a y2", FAR, piece), slot(1, p, FAR, 0, BOTH, piece))
            value = a_y_sum(p, FAR, piece, BOTH)
            pack(p, FAR, 0, BOTH, piece, value)
            keep(p, FAR, 0, BOTH, piece, value)
        send(None, (p, "a side"), out(p, FAR, 0, xh, A0), slot(2, p, FAR, 0, 1 - xh, A0), x_side)
        for r in range(2):
            send(near_here, (p, "a cross", 1 - r), out(p, FAR, 0, r, A1), slot(2, p, FAR, 0, 1 - r, A1), x_cross)

        def a_near():
            for piece in (A0, A1):
                arrived((p, "a y2", NEAR, piece), slot(1, p, NEAR, 0, BOTH, piece))
                pack(p, NEAR, 0, 1, piece, a_y_sum(p, NEAR, piece, 1))
                keep(p, NEAR, 0, 0, piece, a_y_sum(p, NEAR, piece, 0))

        when(near_here, a_near)
        send(near_here, (p, "a near"), out(p, NEAR, 0, 1, A), slot(2, p, NEAR, 0, 0, A), x_side)
        b_y_second(p, NEAR, near_here)

    def hand_on(p, cond, parts):
        def turn():
            whole = jnp.concatenate(parts(), axis=0).T.reshape(2, 64, TOK)
            z_out[p] = whole.astype(BF16)
            if p == 0:
                z_own[...] = whole

        when(cond, turn)
        for e in range(2):
            if (p, e) in z_by:
                send(cond, (p, "z", e), z_out.at[p, z_low if e == 0 else 1 - z_low], z_in.at[p, e], z_by[(p, e)])

    def fourth(p):
        arrived((p, "a side"), slot(2, p, FAR, 0, 1 - xh, A0))

        def far_near():
            pack(p, FAR, 0, 1, A0, have(p, FAR, 0, 1, A0) + came(2, p, FAR, 0, 1, A0))

        def far_far():
            keep(p, FAR, 0, 0, A0, have(p, FAR, 0, 0, A0) + came(2, p, FAR, 0, 0, A0))
            for r in range(2):
                arrived((p, "a cross", r), slot(2, p, FAR, 0, r, A1))
            pack(p, FAR, 0, 1, A1, have(p, FAR, 0, 1, A1) + came(2, p, FAR, 0, 1, A1))
            keep(p, FAR, 0, 0, A1, have(p, FAR, 0, 0, A1) + came(2, p, FAR, 0, 0, A1))

        when(near_here, far_near)
        send(near_here, (p, "a cross2"), out(p, FAR, 0, 1, A0), slot(3, p, FAR, 0, 0, A0), x_cross)
        when(far_here, far_far)
        send(far_here, (p, "a side2"), out(p, FAR, 0, 1, A1), slot(3, p, FAR, 0, 0, A1), x_side)
        b_y_second(p, FAR, far_here)

        def near_parts():
            arrived((p, "a near"), slot(2, p, NEAR, 0, 0, A))
            return [have(p, NEAR, 0, 0, A) + came(2, p, NEAR, 0, 0, A)] + b_final(p, NEAR)

        hand_on(p, near_here, near_parts)

    def fifth(p):
        def far_parts():
            arrived((p, "a cross2"), slot(3, p, FAR, 0, 0, A0))
            arrived((p, "a side2"), slot(3, p, FAR, 0, 0, A1))
            return [have(p, FAR, 0, 0, A) + came(3, p, FAR, 0, 0, A)] + b_final(p, FAR)

        hand_on(p, far_here, far_parts)

    pl.semaphore_wait(barrier, 12)
    t0, t1, t2, t3 = TILES
    for stage, p in (
        (multiply, t0), (multiply, t1), (first, t0), (multiply, t2), (first, t1), (multiply, t3),
        (second, t0), (first, t2), (third, t0), (second, t1), (first, t3), (fourth, t0), (third, t1), (second, t2),
        (fifth, t0), (fourth, t1), (third, t2), (second, t3), (fifth, t1), (fourth, t2), (third, t3),
        (fifth, t2), (fourth, t3), (fifth, t3),
    ):
        stage(p)

    total = z_own[z_low]
    for p in TILES:
        for e in range(2):
            if (p, e) in z_by:
                arrived((p, "z", e), z_in.at[p, e])
                total = total + z_in[p, e].astype(F32)
    out_ref[0] = total.astype(BF16)

    for cond, key, src, dst, peer in pending:
        when(cond, lambda: remote(key, src, dst, peer).wait_send())


def local(residual, enc_weight, dec_weight, latent_ids):
    dec = dec_weight[0].reshape(256, 4, 32, 128).transpose(0, 2, 1, 3).reshape(256, 32, 2, 2, 128)
    ids = latent_ids.transpose(0, 2, 1)
    blocks = (4, 2, 4, 2, TOK, 128)
    return pl.pallas_call(
        kernel,
        out_shape=jax.ShapeDtypeStruct((1, 64, TOK), BF16),
        in_specs=[pl.BlockSpec(memory_space=pl.ANY)] * 4,
        out_specs=pl.BlockSpec(memory_space=pltpu.VMEM),
        scratch_shapes=[
            pltpu.VMEM((TOK, 4096), BF16),
            pltpu.VMEM((4096, 256), BF16),
            pltpu.VMEM((64, TOK), jnp.int32),
            pltpu.VMEM((4, 2, 4, 2, 256, 2, 128), BF16),
            pltpu.VMEM((2, 2 * TOK, 512), BF16),
            pltpu.VMEM(blocks, F32),
            pltpu.VMEM(blocks, BF16),
            pltpu.VMEM(blocks, BF16),
            pltpu.VMEM(blocks, BF16),
            pltpu.VMEM((4,) + blocks, BF16),
            pltpu.VMEM((2, 64, TOK), F32),
            pltpu.VMEM((4, 2, 64, TOK), BF16),
            pltpu.VMEM((4, 2, 64, TOK), BF16),
            pltpu.SemaphoreType.DMA((72,)),
            pltpu.SemaphoreType.DMA((128,)),
            pltpu.SemaphoreType.DMA((128,)),
        ],
        compiler_params=pltpu.CompilerParams(
            collective_id=0, has_side_effects=True, vmem_limit_bytes=60 * 1024 * 1024
        ),
    )(residual, enc_weight, dec, ids)


def solution(mesh):
    in_specs = (
        P("section", None, None),
        P("section", None, "feat"),
        P("section", "feat", None, None),
        P("section", None, None),
    )
    return jax.shard_map(local, mesh=mesh, in_specs=in_specs, out_specs=P("section", "feat", None), check_vma=False)
```

time: 695 us -> 47.7 us (0.07); the launches traced: 683 us -> 47.4 us
  waiting for transfers between devices: 626 us -> 0 us
  Pallas kernels: 0 us -> 46.1 us
  matrix products: 17.1 us -> 0 us
  between operations: 14.1 us -> 0.01 us
  local copies, waits for them, and re-layouts: 11.9 us -> 1.32 us
  blocking collectives: 8.01 us -> 0 us
    unnamed x2 -> x0, waiting for transfers between devices: 626 us -> none
    pallas_call x0 -> x1, Pallas kernels: none -> 46.1 us  [local(): pl.pallas_call(kernel, out_shape=jax.ShapeDtypeStruct((1, 64, TOK), BF16)...]
    dot_general x1 -> x0, matrix products: 17.1 us -> none  [local(): jnp.einsum('nf,flc->cln', latent_acts, weights, preferred_element_type=jn...]
    transpose x1 -> x0, local copies, waits for them, and re-layouts: 9.88 us -> none  [local(): jnp.einsum('nf,flc->cln', latent_acts, weights, preferred_element_type=jn...]
    all_gather x1 -> x0, blocking collectives: 8.01 us -> none  [prefix(): everything = lax.all_gather(shard, axis)]
  transfers between devices with their start and end apart: 1 -> 0, of which waited for: 1 -> 0; matrix products, arithmetic and copies ran while one was open for 0% -> 0% of each run, Pallas kernels for 0% -> 0%
where the time goes in v2:
time: 47.7 us; the launch traced here: 47.4 us
  Pallas kernels  46.1 us (97%)
  local copies, waits for them, and re-layouts  1.32 us (3%)
    pallas_call x1, Pallas kernels, local(): pl.pallas_call(kernel, out_shape=jax.ShapeDtypeStruct((1, 64, TOK), BF16)...  46.1 us
    unnamed x1, local copies, waits for them, and re-layouts  1.32 us

profile of v2, /device:TPU:6, one launch (start us, length us, event | category | flops | bytes accessed | tf_op | source)
XLA Modules:
  0.0 47.4 jit_solution(15634561035261771774)
XLA Ops:
  0.0 46.1 %shard_map.46 = bf16[1,64,128]{2,1,0:T(8,128)(2,1)} custom-call(bf16[1,128,4096]{2,1,0:T(8,128)(2,1)} %res_hbm.1, bf16[1,4096,256]{2,1,0:T(8,128)(2,1)} %enc_hbm.1, bf16[256,32,2,2,128]{4,3,2,1,0:T(2,128)(2,1)} %bitcast.6, s32[1,64,128]{2,1,0:T(8,128)} %bitcast.7), custom_call_target="tpu_custom_call" | custom-call | tf_op jit(solution)/shard_map/pallas_call | solution.py:372
  46.1 1.3 %copy.7 = bf16[1,64,128]{2,1,0:T(8,128)(2,1)} copy(bf16[1,64,128]{2,1,0:T(8,128)(2,1)} %shard_map.46) | data formatting | bytes 32768

commit v3 on v2

v3 whole, which is shorter than its diff:
```python
import jax
import jax.numpy as jnp
from jax import lax
from jax.experimental import pallas as pl
from jax.experimental.pallas import tpu as pltpu
from jax.sharding import PartitionSpec as P

MESH = pl.DeviceIdType.MESH
F32, BF16 = jnp.float32, jnp.bfloat16
TOK = 128
A, B = (0, 64), (64, 64)
NEAR, FAR = 0, 1
TILES = (2, 1, 3, 0)


def when(cond, run):
    if cond is None:
        run()
    else:
        @pl.when(cond)
        def _():
            run()


def rows(piece):
    return pl.ds(piece[0], piece[1])


def kernel(res_hbm, enc_hbm, dec_hbm, ids_hbm, out_ref, res, enc, ids, dec, lhs, acc, core_out, core_in, sent, got,
           z_own, z_out, z_in, load_sem, send_sem, recv_sem):
    section, feat = lax.axis_index("section"), lax.axis_index("feat")
    core, xh = section % 2, section // 2
    y, xl, z = feat // 16, (feat // 8) % 2, feat % 8
    z_pair, z_low = z // 2, z % 2
    flip = {0: y, 1: y + 1 - 2 * (y % 2), 2: (y + 2) % 4, 3: 3 - y}
    near_here, far_here = xh == 0, xh == 1

    def device(core_=core, xh_=xh, y_=y, xl_=xl, z_=z):
        return (xh_ * 2 + core_, (y_ * 2 + xl_) * 8 + z_)

    other_core = device(core_=1 - core)
    y_by = {m: device(y_=flip[m]) for m in range(1, 4)}
    x_side = device(xl_=1 - xl)
    x_cross = device(xh_=1 - xh, xl_=1 - xl)
    x_straight = device(xh_=1 - xh)
    tile_of = {p: (z_pair + p) % 4 for p in TILES}
    z_by = {(p, e): device(z_=2 * tile_of[p] + (z_low if e == 0 else 1 - z_low)) for p in TILES for e in range(2)}
    z_by.pop((0, 0))

    barrier = pltpu.get_barrier_semaphore()
    for peer in [other_core, y_by[1], y_by[2], y_by[3], x_side, x_cross, x_straight] + list(z_by.values()):
        pl.semaphore_signal(barrier, inc=1, device_id=peer, device_id_type=MESH)

    loads = {}

    def load(key, src, dst):
        copy = pltpu.make_async_copy(src, dst, load_sem.at[len(loads)])
        loads[key] = copy
        return copy

    def load_dec(p, t):
        for m in range(4):
            for r in range(2):
                tile = flip[m] * 8 + (xl if r == 0 else 1 - xl) * 4 + tile_of[p]
                load((p, t, m, r), dec_hbm.at[:, tile, t], dec.at[p, t, m, r])
        when(near_here if t == NEAR else None, lambda: [loads[(p, t, m, r)].start() for m in range(4) for r in range(2)])

    load("ids", ids_hbm.at[0], ids).start()
    load("res", res_hbm.at[0], res).start()
    load("enc", enc_hbm.at[0], enc).start()
    for p in TILES:
        load_dec(p, FAR)
        load_dec(p, NEAR)

    for nothing_comes, t in ((section == 0, NEAR), (section == 2, FAR)):
        @pl.when(nothing_comes)
        def _():
            for p in TILES:
                core_in[p, t] = jnp.zeros((4, 2, TOK, 128), BF16)

    loads["ids"].wait()
    local_ids = ids[...] - feat * 256
    latent = lax.broadcasted_iota(jnp.int32, (256, TOK), 0)
    active = latent == local_ids[0:1, :]
    for k in range(1, 64):
        active = active | (latent == local_ids[k:k + 1, :])
    active = jnp.where(active, 1.0, 0.0).astype(F32).T
    spread = (lax.broadcasted_iota(jnp.int32, (256, 512), 1) // 2 == lax.broadcasted_iota(jnp.int32, (256, 512), 0))
    spread = jnp.where(spread, 1.0, 0.0).astype(BF16)
    loads["res"].wait()
    loads["enc"].wait()
    pre_acts = jnp.dot(res[...], enc[...], preferred_element_type=F32)
    acts = (jnp.maximum(pre_acts, 0.0) * active).astype(BF16)
    acts = jnp.dot(acts, spread, preferred_element_type=F32).astype(BF16)
    place = lax.broadcasted_iota(jnp.int32, (TOK, 512), 1) % 2
    for t in range(2):
        for row, low in enumerate((1 - core, core)):
            keep = (place == low) & (2 * t + low >= section)
            lhs[t, pl.ds(row * TOK, TOK), :] = jnp.where(keep, acts, jnp.zeros_like(acts))

    numbers = {}
    pending = []

    def remote(key, src, dst, peer):
        i = numbers.setdefault(key, len(numbers))
        return pltpu.make_async_remote_copy(
            src_ref=src, dst_ref=dst, send_sem=send_sem.at[i], recv_sem=recv_sem.at[i], device_id=peer, device_id_type=MESH
        )

    def send(cond, key, src, dst, peer):
        when(cond, lambda: remote(key, src, dst, peer).start())
        pending.append((cond, key, src, dst, peer))

    def arrived(key, region):
        remote(key, region, region, other_core).wait_recv()

    ALL, BOTH = pl.ds(0, 4), pl.ds(0, 2)

    def out(p, t, m, r, piece):
        return sent.at[p, t, m, r, rows(piece), :]

    def slot(step, p, t, m, r, piece):
        return got.at[step, p, t, m, r, rows(piece), :]

    def have(p, t, m, r, piece):
        return acc[p, t, m, r, rows(piece), :]

    def came(step, p, t, m, r, piece):
        return got[step, p, t, m, r, rows(piece), :].astype(F32)

    def keep(p, t, m, r, piece, value):
        acc[p, t, m, r, rows(piece), :] = value

    def pack(p, t, m, r, piece, value):
        sent[p, t, m, r, rows(piece), :] = value.astype(BF16)

    def multiply(p):
        def one(t):
            for m in range(4):
                for r in range(2):
                    loads[(p, t, m, r)].wait()
            for m in range(4):
                w = jnp.concatenate([dec.at[p, t, m, r].reshape(512, 128)[...] for r in range(2)], axis=1)
                both = jnp.dot(lhs[t], w, preferred_element_type=F32)
                for r in range(2):
                    core_out[p, t, m, r] = both[0:TOK, r * 128:(r + 1) * 128].astype(BF16)
                    acc[p, t, m, r] = both[TOK:2 * TOK, r * 128:(r + 1) * 128]

        one(FAR)
        send(section != 3, (p, "core", FAR), core_out.at[p, FAR], core_in.at[p, FAR], other_core)
        when(near_here, lambda: one(NEAR))
        send(section == 0, (p, "core", NEAR), core_out.at[p, NEAR], core_in.at[p, NEAR], other_core)

    def first(p):
        def core_sum(t, m, r, piece):
            return have(p, t, m, r, piece) + core_in[p, t, m, r, rows(piece), :].astype(F32)

        def a_rows(t):
            for m in range(1, 4):
                pack(p, t, m, BOTH, A, core_sum(t, m, BOTH, A))
            keep(p, t, 0, BOTH, A, core_sum(t, 0, BOTH, A))

        def b_rows(t):
            for m in range(4):
                pack(p, t, m, 1, B, core_sum(t, m, 1, B))
            if t == NEAR:
                for m in range(4):
                    keep(p, t, m, 0, B, core_sum(t, m, 0, B))
            else:
                @pl.when(near_here)
                def _():
                    for m in range(4):
                        pack(p, t, m, 0, B, core_sum(t, m, 0, B))

                @pl.when(far_here)
                def _():
                    for m in range(4):
                        keep(p, t, m, 0, B, core_sum(t, m, 0, B))

        def y_out(cond, t):
            for m in (2, 1, 3):
                send(cond, (p, "a y", t, m), out(p, t, m, BOTH, A), slot(0, p, t, m, BOTH, A), y_by[m])

        when(section != 2, lambda: arrived((p, "core", FAR), core_in.at[p, FAR]))
        b_rows(FAR)
        x_out(p, "b", FAR, ALL, B, (0, 1, 2))
        a_rows(FAR)
        y_out(None, FAR)
        when(section == 1, lambda: arrived((p, "core", NEAR), core_in.at[p, NEAR]))
        when(near_here, lambda: b_rows(NEAR))
        x_out(p, "b", NEAR, ALL, B, (0, 1, 2))
        when(near_here, lambda: a_rows(NEAR))
        y_out(near_here, NEAR)

    def x_out(p, name, t, m, piece, steps):
        side, cross, straight = steps
        if t == NEAR:
            send(near_here, (p, name, "near"), out(p, t, m, 1, piece), slot(side, p, t, m, 0, piece), x_side)
        else:
            send(near_here, (p, name, "straight"), out(p, t, m, 0, piece), slot(straight, p, t, m, 0, piece), x_straight)
            send(near_here, (p, name, "cross"), out(p, t, m, 1, piece), slot(cross, p, t, m, 0, piece), x_cross)
            send(far_here, (p, name, "side"), out(p, t, m, 1, piece), slot(side, p, t, m, 0, piece), x_side)

    def x_in(p, name, t, m, piece, steps):
        side, cross, straight = steps
        if t == NEAR:
            arrived((p, name, "near"), slot(side, p, t, m, 0, piece))
        else:
            arrived((p, name, "side"), slot(side, p, t, m, 0, piece))
            arrived((p, name, "cross"), slot(cross, p, t, m, 0, piece))
            arrived((p, name, "straight"), slot(straight, p, t, m, 0, piece))

    def x_sum(p, t, m, piece, steps):
        value = have(p, t, m, 0, piece)
        for step in steps[:1] if t == NEAR else steps:
            value = value + came(step, p, t, m, 0, piece)
        return value

    def second(p):
        def b_own(t):
            x_in(p, "b", t, ALL, B, (0, 1, 2))
            for m in range(1, 4):
                pack(p, t, m, 0, B, x_sum(p, t, m, B, (0, 1, 2)))
            keep(p, t, 0, 0, B, x_sum(p, t, 0, B, (0, 1, 2)))

        def a_sum(t, r):
            value = have(p, t, 0, r, A)
            for m in range(1, 4):
                value = value + came(0, p, t, m, r, A)
            return value

        def a_in(t):
            for m in range(1, 4):
                arrived((p, "a y", t, m), slot(0, p, t, m, BOTH, A))

        def a_far():
            a_in(FAR)
            pack(p, FAR, 0, 1, A, a_sum(FAR, 1))
            when(near_here, lambda: pack(p, FAR, 0, 0, A, a_sum(FAR, 0)))
            when(far_here, lambda: keep(p, FAR, 0, 0, A, a_sum(FAR, 0)))

        def a_near():
            a_in(NEAR)
            pack(p, NEAR, 0, 1, A, a_sum(NEAR, 1))
            keep(p, NEAR, 0, 0, A, a_sum(NEAR, 0))

        def y_out(cond, t):
            for m in (2, 1, 3):
                send(cond, (p, "b y", m), out(p, t, m, 0, B), slot(3, p, t, m, 0, B), y_by[m])

        a_far()
        x_out(p, "a", FAR, 0, A, (1, 2, 3))
        when(far_here, lambda: b_own(FAR))
        y_out(far_here, FAR)
        when(near_here, lambda: b_own(NEAR))
        y_out(near_here, NEAR)
        when(near_here, a_near)
        x_out(p, "a", NEAR, 0, A, (1, 2, 3))

    def third(p):
        def parts(t):
            x_in(p, "a", t, 0, A, (1, 2, 3))
            upper = x_sum(p, t, 0, A, (1, 2, 3))
            lower = have(p, t, 0, 0, B)
            for m in range(1, 4):
                arrived((p, "b y", m), slot(3, p, t, m, 0, B))
                lower = lower + came(3, p, t, m, 0, B)
            whole = jnp.concatenate([upper, lower], axis=0).T.reshape(2, 64, TOK)
            z_out[p] = whole.astype(BF16)
            if p == 0:
                z_own[...] = whole

        when(near_here, lambda: parts(NEAR))
        when(far_here, lambda: parts(FAR))
        for e in range(2):
            if (p, e) in z_by:
                send(None, (p, "z", e), z_out.at[p, z_low if e == 0 else 1 - z_low], z_in.at[p, e], z_by[(p, e)])

    pl.semaphore_wait(barrier, 14)
    t0, t1, t2, t3 = TILES
    for stage, p in (
        (multiply, t0), (multiply, t1), (first, t0), (multiply, t2), (first, t1), (multiply, t3), (first, t2), (first, t3),
        (second, t0), (second, t1), (second, t2), (third, t0), (second, t3), (third, t1), (third, t2), (third, t3),
    ):
        stage(p)

    total = z_own[z_low]
    for p in TILES:
        for e in range(2):
            if (p, e) in z_by:
                arrived((p, "z", e), z_in.at[p, e])
                total = total + z_in[p, e].astype(F32)
    out_ref[0] = total.astype(BF16)

    for cond, key, src, dst, peer in pending:
        when(cond, lambda: remote(key, src, dst, peer).wait_send())


def local(residual, enc_weight, dec_weight, latent_ids):
    dec = dec_weight[0].reshape(256, 4, 32, 128).transpose(0, 2, 1, 3).reshape(256, 32, 2, 2, 128)
    ids = latent_ids.transpose(0, 2, 1)
    blocks = (4, 2, 4, 2, TOK, 128)
    return pl.pallas_call(
        kernel,
        out_shape=jax.ShapeDtypeStruct((1, 64, TOK), BF16),
        in_specs=[pl.BlockSpec(memory_space=pl.ANY)] * 4,
        out_specs=pl.BlockSpec(memory_space=pltpu.VMEM),
        scratch_shapes=[
            pltpu.VMEM((TOK, 4096), BF16),
            pltpu.VMEM((4096, 256), BF16),
            pltpu.VMEM((64, TOK), jnp.int32),
            pltpu.VMEM((4, 2, 4, 2, 256, 2, 128), BF16),
            pltpu.VMEM((2, 2 * TOK, 512), BF16),
            pltpu.VMEM(blocks, F32),
            pltpu.VMEM(blocks, BF16),
            pltpu.VMEM(blocks, BF16),
            pltpu.VMEM(blocks, BF16),
            pltpu.VMEM((4,) + blocks, BF16),
            pltpu.VMEM((2, 64, TOK), F32),
            pltpu.VMEM((4, 2, 64, TOK), BF16),
            pltpu.VMEM((4, 2, 64, TOK), BF16),
            pltpu.SemaphoreType.DMA((72,)),
            pltpu.SemaphoreType.DMA((128,)),
            pltpu.SemaphoreType.DMA((128,)),
        ],
        compiler_params=pltpu.CompilerParams(
            collective_id=0, has_side_effects=True, vmem_limit_bytes=60 * 1024 * 1024
        ),
    )(residual, enc_weight, dec, ids)


def solution(mesh):
    in_specs = (
        P("section", None, None),
        P("section", None, "feat"),
        P("section", "feat", None, None),
        P("section", None, None),
    )
    return jax.shard_map(local, mesh=mesh, in_specs=in_specs, out_specs=P("section", "feat", None), check_vma=False)
```

time: 47.7 us -> 37.6 us (0.79)
  Pallas kernels: 46.1 us -> 36 us
    pallas_call x1, Pallas kernels: 46.1 us -> 36 us  [local(): pl.pallas_call(kernel, out_shape=jax.ShapeDtypeStruct((1, 64, TOK), BF16)...]
where the time goes in v3:
time: 37.6 us; the launch traced here: 37.4 us
  Pallas kernels  36 us (96%)
  local copies, waits for them, and re-layouts  1.32 us (4%)
    pallas_call x1, Pallas kernels, local(): pl.pallas_call(kernel, out_shape=jax.ShapeDtypeStruct((1, 64, TOK), BF16)...  36 us
    unnamed x1, local copies, waits for them, and re-layouts  1.32 us

profile of v3, /device:TPU:6, one launch (start us, length us, event | category | flops | bytes accessed | tf_op | source)
XLA Modules:
  0.0 37.4 jit_solution(9733798678069419945)
XLA Ops:
  0.0 36.0 %shard_map.46 = bf16[1,64,128]{2,1,0:T(8,128)(2,1)} custom-call(bf16[1,128,4096]{2,1,0:T(8,128)(2,1)} %res_hbm.1, bf16[1,4096,256]{2,1,0:T(8,128)(2,1)} %enc_hbm.1, bf16[256,32,2,2,128]{4,3,2,1,0:T(2,128)(2,1)} %bitcast.6, s32[1,64,128]{2,1,0:T(8,128)} %bitcast.7), custom_call_target="tpu_custom_call" | custom-call | tf_op jit(solution)/shard_map/pallas_call | solution.py:303
  36.0 1.3 %copy.7 = bf16[1,64,128]{2,1,0:T(8,128)(2,1)} copy(bf16[1,64,128]{2,1,0:T(8,128)(2,1)} %shard_map.46) | data formatting | bytes 32768

commit v4 on v3

--- a/solution.py
+++ b/solution.py
@@ -8,7 +8,8 @@
 MESH = pl.DeviceIdType.MESH
 F32, BF16 = jnp.float32, jnp.bfloat16
 TOK = 128
-A, B = (0, 64), (64, 64)
+A, B = ((0, 48), (0, 80)), ((48, 80), (80, 48))
+SPLIT = (((0, 16), (16, 32)), ((0, 48), (48, 32)))
 NEAR, FAR = 0, 1
 TILES = (2, 1, 3, 0)
 
@@ -66,17 +67,13 @@
         when(near_here if t == NEAR else None, lambda: [loads[(p, t, m, r)].start() for m in range(4) for r in range(2)])
 
     load("ids", ids_hbm.at[0], ids).start()
-    load("res", res_hbm.at[0], res).start()
-    load("enc", enc_hbm.at[0], enc).start()
+    for c in range(4):
+        part = pl.ds(c * 1024, 1024)
+        load(("res", c), res_hbm.at[0, :, part], res.at[:, part]).start()
+        load(("enc", c), enc_hbm.at[0, part, :], enc.at[part, :]).start()
     for p in TILES:
         load_dec(p, FAR)
         load_dec(p, NEAR)
-
-    for nothing_comes, t in ((section == 0, NEAR), (section == 2, FAR)):
-        @pl.when(nothing_comes)
-        def _():
-            for p in TILES:
-                core_in[p, t] = jnp.zeros((4, 2, TOK, 128), BF16)
 
     loads["ids"].wait()
     local_ids = ids[...] - feat * 256
@@ -87,9 +84,12 @@
     active = jnp.where(active, 1.0, 0.0).astype(F32).T
     spread = (lax.broadcasted_iota(jnp.int32, (256, 512), 1) // 2 == lax.broadcasted_iota(jnp.int32, (256, 512), 0))
     spread = jnp.where(spread, 1.0, 0.0).astype(BF16)
-    loads["res"].wait()
-    loads["enc"].wait()
-    pre_acts = jnp.dot(res[...], enc[...], preferred_element_type=F32)
+    pre_acts = jnp.zeros((TOK, 256), F32)
+    for c in range(4):
+        part = pl.ds(c * 1024, 1024)
+        loads[("res", c)].wait()
+        loads[("enc", c)].wait()
+        pre_acts = pre_acts + jnp.dot(res[:, part], enc[part, :], preferred_element_type=F32)
     acts = (jnp.maximum(pre_acts, 0.0) * active).astype(BF16)
     acts = jnp.dot(acts, spread, preferred_element_type=F32).astype(BF16)
     place = lax.broadcasted_iota(jnp.int32, (TOK, 512), 1) % 2
@@ -134,7 +134,7 @@
     def pack(p, t, m, r, piece, value):
         sent[p, t, m, r, rows(piece), :] = value.astype(BF16)
 
-    def multiply(p):
+    def multiply(p, far):
         def one(t):
             for m in range(4):
                 for r in range(2):
@@ -146,51 +146,108 @@
                     core_out[p, t, m, r] = both[0:TOK, r * 128:(r + 1) * 128].astype(BF16)
                     acc[p, t, m, r] = both[TOK:2 * TOK, r * 128:(r + 1) * 128]
 
-        one(FAR)
-        send(section != 3, (p, "core", FAR), core_out.at[p, FAR], core_in.at[p, FAR], other_core)
+        if far:
+            one(FAR)
+            send(section != 3, (p, "core", FAR), core_out.at[p, FAR], core_in.at[p, FAR], other_core)
+            return
         when(near_here, lambda: one(NEAR))
         send(section == 0, (p, "core", NEAR), core_out.at[p, NEAR], core_in.at[p, NEAR], other_core)
 
-    def first(p):
+    PATHS = ((1, 1, 3), (3, 2, 1))
+    SLOT_OF = ((0, 3), (1, 0))
+
+    def halving(p):
+        return p != 0
+
+    def a_rows(p, t, core_sum):
+        if not halving(p):
+            for m in range(1, 4):
+                pack(p, t, m, BOTH, A[t], core_sum(t, m, BOTH, A[t]))
+            keep(p, t, 0, BOTH, A[t], core_sum(t, 0, BOTH, A[t]))
+            return
+        for path, piece in zip(PATHS, SPLIT[t]):
+            for m in range(4):
+                (pack if m in (path[1], path[1] + 1) else keep)(p, t, m, BOTH, piece, core_sum(t, m, BOTH, piece))
+
+    def a_y_out(p, cond, t):
+        if not halving(p):
+            for m in (2, 1, 3):
+                send(cond, (p, "a y", t, m), out(p, t, m, BOTH, A[t]), slot(0, p, t, m, BOTH, A[t]), y_by[m])
+            return
+        for path, piece in zip(PATHS, SPLIT[t]):
+            send(cond, (p, "a y1", t, path), sent.at[p, t, pl.ds(path[1], 2), BOTH, rows(piece), :],
+                 got.at[0, p, t, BOTH, BOTH, rows(piece), :], y_by[path[0]])
+
+    def middle(p):
+        def one(t):
+            for path, piece, slots in zip(PATHS, SPLIT[t], SLOT_OF):
+                k = path[2]
+                arrived((p, "a y1", t, path), got.at[0, p, t, BOTH, BOTH, rows(piece), :])
+                pack(p, t, k, BOTH, piece, have(p, t, k, BOTH, piece) + came(0, p, t, slots.index(k), BOTH, piece))
+
+        for t, cond in ((FAR, None), (NEAR, near_here)):
+            when(cond, lambda: one(t))
+            for path, piece in zip(PATHS, SPLIT[t]):
+                k = path[2]
+                send(cond, (p, "a y2", t, path), out(p, t, k, BOTH, piece), slot(0, p, t, 3, BOTH, piece), y_by[k])
+
+    def a_in(p, t):
+        if not halving(p):
+            for m in range(1, 4):
+                arrived((p, "a y", t, m), slot(0, p, t, m, BOTH, A[t]))
+            return
+        for path, piece in zip(PATHS, SPLIT[t]):
+            arrived((p, "a y2", t, path), slot(0, p, t, 3, BOTH, piece))
+
+    def a_each(p, t, r, put):
+        if not halving(p):
+            value = have(p, t, 0, r, A[t])
+            for m in range(1, 4):
+                value = value + came(0, p, t, m, r, A[t])
+            put(p, t, 0, r, A[t], value)
+            return
+        for piece, slots in zip(SPLIT[t], SLOT_OF):
+            value = have(p, t, 0, r, piece) + came(0, p, t, slots.index(0), r, piece) + came(0, p, t, 3, r, piece)
+            put(p, t, 0, r, piece, value)
+
+    def first(p, far):
+        def nothing_came(t):
+            core_in[p, t] = jnp.zeros((4, 2, TOK, 128), BF16)
+
         def core_sum(t, m, r, piece):
             return have(p, t, m, r, piece) + core_in[p, t, m, r, rows(piece), :].astype(F32)
 
-        def a_rows(t):
-            for m in range(1, 4):
-                pack(p, t, m, BOTH, A, core_sum(t, m, BOTH, A))
-            keep(p, t, 0, BOTH, A, core_sum(t, 0, BOTH, A))
-
         def b_rows(t):
             for m in range(4):
-                pack(p, t, m, 1, B, core_sum(t, m, 1, B))
+                pack(p, t, m, 1, B[t], core_sum(t, m, 1, B[t]))
             if t == NEAR:
                 for m in range(4):
-                    keep(p, t, m, 0, B, core_sum(t, m, 0, B))
+                    keep(p, t, m, 0, B[t], core_sum(t, m, 0, B[t]))
             else:
                 @pl.when(near_here)
                 def _():
                     for m in range(4):
-                        pack(p, t, m, 0, B, core_sum(t, m, 0, B))
+                        pack(p, t, m, 0, B[t], core_sum(t, m, 0, B[t]))
 
                 @pl.when(far_here)
                 def _():
                     for m in range(4):
-                        keep(p, t, m, 0, B, core_sum(t, m, 0, B))
-
-        def y_out(cond, t):
-            for m in (2, 1, 3):
-                send(cond, (p, "a y", t, m), out(p, t, m, BOTH, A), slot(0, p, t, m, BOTH, A), y_by[m])
-
-        when(section != 2, lambda: arrived((p, "core", FAR), core_in.at[p, FAR]))
-        b_rows(FAR)
-        x_out(p, "b", FAR, ALL, B, (0, 1, 2))
-        a_rows(FAR)
-        y_out(None, FAR)
+                        keep(p, t, m, 0, B[t], core_sum(t, m, 0, B[t]))
+
+        if far:
+            when(section != 2, lambda: arrived((p, "core", FAR), core_in.at[p, FAR]))
+            when(section == 2, lambda: nothing_came(FAR))
+            b_rows(FAR)
+            x_out(p, "b", FAR, ALL, B[FAR], (0, 1, 2))
+            a_rows(p, FAR, core_sum)
+            a_y_out(p, None, FAR)
+            return
         when(section == 1, lambda: arrived((p, "core", NEAR), core_in.at[p, NEAR]))
+        when(section == 0, lambda: nothing_came(NEAR))
         when(near_here, lambda: b_rows(NEAR))
-        x_out(p, "b", NEAR, ALL, B, (0, 1, 2))
-        when(near_here, lambda: a_rows(NEAR))
-        y_out(near_here, NEAR)
+        x_out(p, "b", NEAR, ALL, B[NEAR], (0, 1, 2))
+        when(near_here, lambda: a_rows(p, NEAR, core_sum))
+        a_y_out(p, near_here, NEAR)
 
     def x_out(p, name, t, m, piece, steps):
         side, cross, straight = steps
@@ -218,53 +275,43 @@
 
     def second(p):
         def b_own(t):
-            x_in(p, "b", t, ALL, B, (0, 1, 2))
-            for m in range(1, 4):
-                pack(p, t, m, 0, B, x_sum(p, t, m, B, (0, 1, 2)))
-            keep(p, t, 0, 0, B, x_sum(p, t, 0, B, (0, 1, 2)))
-
-        def a_sum(t, r):
-            value = have(p, t, 0, r, A)
-            for m in range(1, 4):
-                value = value + came(0, p, t, m, r, A)
-            return value
-
-        def a_in(t):
-            for m in range(1, 4):
-                arrived((p, "a y", t, m), slot(0, p, t, m, BOTH, A))
+            x_in(p, "b", t, ALL, B[t], (0, 1, 2))
+            for m in range(1, 4):
+                pack(p, t, m, 0, B[t], x_sum(p, t, m, B[t], (0, 1, 2)))
+            keep(p, t, 0, 0, B[t], x_sum(p, t, 0, B[t], (0, 1, 2)))
 
         def a_far():
-            a_in(FAR)
-            pack(p, FAR, 0, 1, A, a_sum(FAR, 1))
-            when(near_here, lambda: pack(p, FAR, 0, 0, A, a_sum(FAR, 0)))
-            when(far_here, lambda: keep(p, FAR, 0, 0, A, a_sum(FAR, 0)))
+            a_in(p, FAR)
+            a_each(p, FAR, 1, pack)
+            when(near_here, lambda: a_each(p, FAR, 0, pack))
+            when(far_here, lambda: a_each(p, FAR, 0, keep))
 
         def a_near():
-            a_in(NEAR)
-            pack(p, NEAR, 0, 1, A, a_sum(NEAR, 1))
-            keep(p, NEAR, 0, 0, A, a_sum(NEAR, 0))
+            a_in(p, NEAR)
+            a_each(p, NEAR, 1, pack)
+            a_each(p, NEAR, 0, keep)
 
         def y_out(cond, t):
             for m in (2, 1, 3):
-                send(cond, (p, "b y", m), out(p, t, m, 0, B), slot(3, p, t, m, 0, B), y_by[m])
+                send(cond, (p, "b y", m), out(p, t, m, 0, B[t]), slot(3, p, t, m, 0, B[t]), y_by[m])
 
         a_far()
-        x_out(p, "a", FAR, 0, A, (1, 2, 3))
+        x_out(p, "a", FAR, 0, A[FAR], (1, 2, 3))
         when(far_here, lambda: b_own(FAR))
         y_out(far_here, FAR)
         when(near_here, lambda: b_own(NEAR))
         y_out(near_here, NEAR)
         when(near_here, a_near)
-        x_out(p, "a", NEAR, 0, A, (1, 2, 3))
+        x_out(p, "a", NEAR, 0, A[NEAR], (1, 2, 3))
 
     def third(p):
         def parts(t):
-            x_in(p, "a", t, 0, A, (1, 2, 3))
-            upper = x_sum(p, t, 0, A, (1, 2, 3))
-            lower = have(p, t, 0, 0, B)
-            for m in range(1, 4):
-                arrived((p, "b y", m), slot(3, p, t, m, 0, B))
-                lower = lower + came(3, p, t, m, 0, B)
+            x_in(p, "a", t, 0, A[t], (1, 2, 3))
+            upper = x_sum(p, t, 0, A[t], (1, 2, 3))
+            lower = have(p, t, 0, 0, B[t])
+            for m in range(1, 4):
+                arrived((p, "b y", m), slot(3, p, t, m, 0, B[t]))
+                lower = lower + came(3, p, t, m, 0, B[t])
             whole = jnp.concatenate([upper, lower], axis=0).T.reshape(2, 64, TOK)
             z_out[p] = whole.astype(BF16)
             if p == 0:
@@ -278,11 +325,14 @@
 
     pl.semaphore_wait(barrier, 14)
     t0, t1, t2, t3 = TILES
-    for stage, p in (
-        (multiply, t0), (multiply, t1), (first, t0), (multiply, t2), (first, t1), (multiply, t3), (first, t2), (first, t3),
+    for stage, *at in (
+        (multiply, t0, True), (multiply, t0, False), (multiply, t1, True), (first, t0, True),
+        (multiply, t1, False), (first, t0, False), (multiply, t2, True), (first, t1, True),
+        (multiply, t2, False), (first, t1, False), (multiply, t3, True), (multiply, t3, False), (middle, t0),
+        (first, t2, True), (first, t2, False), (middle, t1), (first, t3, True), (first, t3, False), (middle, t2),
         (second, t0), (second, t1), (second, t2), (third, t0), (second, t3), (third, t1), (third, t2), (third, t3),
     ):
-        stage(p)
+        stage(*at)
 
     total = z_own[z_low]
     for p in TILES:
@@ -319,7 +369,7 @@
             pltpu.VMEM((2, 64, TOK), F32),
             pltpu.VMEM((4, 2, 64, TOK), BF16),
             pltpu.VMEM((4, 2, 64, TOK), BF16),
-            pltpu.SemaphoreType.DMA((72,)),
+            pltpu.SemaphoreType.DMA((80,)),
             pltpu.SemaphoreType.DMA((128,)),
             pltpu.SemaphoreType.DMA((128,)),
         ],

time: 37.6 us -> 37 us (0.984)
  Pallas kernels: 36 us -> 35.5 us
    pallas_call x1, Pallas kernels: 36 us -> 35.5 us  [local(): pl.pallas_call(kernel, out_shape=jax.ShapeDtypeStruct((1, 64, TOK), BF16)...]
where the time goes in v4:
time: 37 us; the launch traced here: 36.8 us
  Pallas kernels  35.5 us (96%)
  local copies, waits for them, and re-layouts  1.32 us (4%)
    pallas_call x1, Pallas kernels, local(): pl.pallas_call(kernel, out_shape=jax.ShapeDtypeStruct((1, 64, TOK), BF16)...  35.5 us
    unnamed x1, local copies, waits for them, and re-layouts  1.32 us

profile of v4, /device:TPU:6, one launch (start us, length us, event | category | flops | bytes accessed | tf_op | source)
XLA Modules:
  0.0 36.8 jit_solution(5249233626562994120)
XLA Ops:
  0.0 35.5 %shard_map.46 = bf16[1,64,128]{2,1,0:T(8,128)(2,1)} custom-call(bf16[1,128,4096]{2,1,0:T(8,128)(2,1)} %res_hbm.1, bf16[1,4096,256]{2,1,0:T(8,128)(2,1)} %enc_hbm.1, bf16[256,32,2,2,128]{4,3,2,1,0:T(2,128)(2,1)} %bitcast.6, s32[1,64,128]{2,1,0:T(8,128)} %bitcast.7), custom_call_target="tpu_custom_call" | custom-call | tf_op jit(solution)/shard_map/pallas_call | solution.py:353
  35.5 1.3 %copy.7 = bf16[1,64,128]{2,1,0:T(8,128)(2,1)} copy(bf16[1,64,128]{2,1,0:T(8,128)(2,1)} %shard_map.46) | data formatting | bytes 32768

commit v5 on v4

--- a/solution.py
+++ b/solution.py
@@ -323,6 +323,11 @@
             if (p, e) in z_by:
                 send(None, (p, "z", e), z_out.at[p, z_low if e == 0 else 1 - z_low], z_in.at[p, e], z_by[(p, e)])
 
+    def drain(along_z):
+        for cond, key, src, dst, peer in pending:
+            if (key[1] == "z") == along_z:
+                when(cond, lambda: remote(key, src, dst, peer).wait_send())
+
     pl.semaphore_wait(barrier, 14)
     t0, t1, t2, t3 = TILES
     for stage, *at in (
@@ -332,6 +337,8 @@
         (first, t2, True), (first, t2, False), (middle, t1), (first, t3, True), (first, t3, False), (middle, t2),
         (second, t0), (second, t1), (second, t2), (third, t0), (second, t3), (third, t1), (third, t2), (third, t3),
     ):
+        if at == [t3] and stage is third:
+            drain(False)
         stage(*at)
 
     total = z_own[z_low]
@@ -342,8 +349,7 @@
                 total = total + z_in[p, e].astype(F32)
     out_ref[0] = total.astype(BF16)
 
-    for cond, key, src, dst, peer in pending:
-        when(cond, lambda: remote(key, src, dst, peer).wait_send())
+    drain(True)
 
 
 def local(residual, enc_weight, dec_weight, latent_ids):

time: 37 us -> 36.9 us (level)
  no operation moved by 1% of the time
where the time goes in v5:
time: 36.9 us; the launch traced here: 36.7 us
  Pallas kernels  35.4 us (96%)
  local copies, waits for them, and re-layouts  1.32 us (4%)
    pallas_call x1, Pallas kernels, local(): pl.pallas_call(kernel, out_shape=jax.ShapeDtypeStruct((1, 64, TOK), BF16)...  35.4 us
    unnamed x1, local copies, waits for them, and re-layouts  1.32 us

profile of v5, /device:TPU:6, one launch (start us, length us, event | category | flops | bytes accessed | tf_op | source)
XLA Modules:
  0.0 36.7 jit_solution(2903834034754174004)
XLA Ops:
  0.0 35.4 %shard_map.46 = bf16[1,64,128]{2,1,0:T(8,128)(2,1)} custom-call(bf16[1,128,4096]{2,1,0:T(8,128)(2,1)} %res_hbm.1, bf16[1,4096,256]{2,1,0:T(8,128)(2,1)} %enc_hbm.1, bf16[256,32,2,2,128]{4,3,2,1,0:T(2,128)(2,1)} %bitcast.6, s32[1,64,128]{2,1,0:T(8,128)} %bitcast.7), custom_call_target="tpu_custom_call" | custom-call | tf_op jit(solution)/shard_map/pallas_call | solution.py:359
  35.4 1.3 %copy.7 = bf16[1,64,128]{2,1,0:T(8,128)(2,1)} copy(bf16[1,64,128]{2,1,0:T(8,128)(2,1)} %shard_map.46) | data formatting | bytes 32768

commit v6 on v4

--- a/solution.py
+++ b/solution.py
@@ -8,8 +8,8 @@
 MESH = pl.DeviceIdType.MESH
 F32, BF16 = jnp.float32, jnp.bfloat16
 TOK = 128
-A, B = ((0, 48), (0, 80)), ((48, 80), (80, 48))
-SPLIT = (((0, 16), (16, 32)), ((0, 48), (48, 32)))
+A, B = ((0, 64), (0, 64)), ((64, 64), (64, 64))
+SPLIT = (((0, 32), (32, 32)), ((0, 32), (32, 32)))
 NEAR, FAR = 0, 1
 TILES = (2, 1, 3, 0)
 

time: 37 us -> 37.1 us (level)
  no operation moved by 1% of the time
where the time goes in v6:
time: 37.1 us; the launch traced here: 36.9 us
  Pallas kernels  35.6 us (96%)
  local copies, waits for them, and re-layouts  1.32 us (4%)
    pallas_call x1, Pallas kernels, local(): pl.pallas_call(kernel, out_shape=jax.ShapeDtypeStruct((1, 64, TOK), BF16)...  35.6 us
    unnamed x1, local copies, waits for them, and re-layouts  1.32 us

profile of v6, /device:TPU:6, one launch (start us, length us, event | category | flops | bytes accessed | tf_op | source)
XLA Modules:
  0.0 36.9 jit_solution(1045577247100348890)
XLA Ops:
  0.0 35.6 %shard_map.46 = bf16[1,64,128]{2,1,0:T(8,128)(2,1)} custom-call(bf16[1,128,4096]{2,1,0:T(8,128)(2,1)} %res_hbm.1, bf16[1,4096,256]{2,1,0:T(8,128)(2,1)} %enc_hbm.1, bf16[256,32,2,2,128]{4,3,2,1,0:T(2,128)(2,1)} %bitcast.6, s32[1,64,128]{2,1,0:T(8,128)} %bitcast.7), custom_call_target="tpu_custom_call" | custom-call | tf_op jit(solution)/shard_map/pallas_call | solution.py:353
  35.6 1.3 %copy.7 = bf16[1,64,128]{2,1,0:T(8,128)(2,1)} copy(bf16[1,64,128]{2,1,0:T(8,128)(2,1)} %shard_map.46) | data formatting | bytes 32768
